TPU v7x, 256 devices: a whole 4x4x8 slice. The times are simulated.
256 devices in a mesh: src: 32 (over z, y), tgt: 8 (over x, core).
Axes of the slice: x: 4, y: 4, z: 8, core: 2. Of those that a mesh axis runs over, the one named last changes fastest.
Arguments:
- source: bfloat16 [32768, 300], P('src'), may hold values from -70 to 70
- target: bfloat16 [16384, 300], P('tgt'), may hold values from -11 to 11
- start_map: float32 [300, 300], replicated, may hold values from -1.5 to 1.5
Outputs:
- source_soft: bfloat16 [32768, 300], P(('src', 'tgt'))
- target_soft: bfloat16 [16384, 300], P('tgt')
- polar_map: float32 [300, 300], replicated
All inputs are finite; a program needn't handle non-finite values.
Results may differ from a plain program's by a relative error of at most 0.014.
The roundings to bfloat16 on the way count: a program that leaves them out, or rounds other values in their place, can miss the bound.
Values may be sent and summed in bfloat16 or wider, within the bound.
A program may use at most 64 MiB of HBM per device.

v0:
```python
import math
import jax
import jax.numpy as jnp
from jax import lax
from jax.sharding import PartitionSpec as P

ITERS = 2
NEWTON_STEPS = 8


def polar_steps(covariance):
    highest = lax.Precision.HIGHEST
    current = covariance / jnp.sqrt(jnp.sum(covariance * covariance) + 1e-06)
    for newton in range(NEWTON_STEPS):
        gram_matrix = jnp.dot(current.T, current, precision=highest)
        current = 1.5 * current - 0.5 * jnp.dot(current, gram_matrix, precision=highest)
    return current


def translation_sums(row_weights, col_weights, source, target, share_target, src_index):
    source_sum = lax.psum_scatter(
        jnp.dot(row_weights, target, preferred_element_type=jnp.float32),
        "tgt",
        scatter_dimension=0,
        tiled=True,
    )
    target_full = lax.psum(
        lax.dot_general(
            col_weights, source, (((0,), (0,)), ((), ())), preferred_element_type=jnp.float32
        ),
        "src",
    )
    target_sum = lax.dynamic_slice_in_dim(target_full, src_index * share_target, share_target, 0)
    return (source_sum, target_sum, target_full)


def body(source, target, start_map):
    highest = lax.Precision.HIGHEST
    score_scale = 2.0 / math.sqrt(source.shape[1])
    rows_source = source.shape[0]
    rows_target = target.shape[0]
    src_devices = lax.axis_size("src")
    tgt_devices = lax.axis_size("tgt")
    src_index = lax.axis_index("src")
    tgt_index = lax.axis_index("tgt")
    share_source = rows_source // tgt_devices
    share_target = rows_target // src_devices
    source_piece = lax.dynamic_slice_in_dim(
        source, tgt_index * share_source, share_source, 0
    ).astype(jnp.float32)
    target_piece = lax.dynamic_slice_in_dim(
        target, src_index * share_target, share_target, 0
    ).astype(jnp.float32)
    current = start_map
    source_sum = None
    target_sum = None
    target_full = None
    for iteration in range(ITERS):
        mapped = jnp.dot(
            source, current.astype(jnp.bfloat16), preferred_element_type=jnp.float32
        ).astype(jnp.bfloat16)
        scores = (
            lax.dot_general(
                mapped, target, (((1,), (1,)), ((), ())), preferred_element_type=jnp.float32
            )
            * score_scale
        )
        row_local = jnp.max(scores, axis=1)
        col_local = jnp.max(scores, axis=0)
        row_top = lax.pmax(row_local, "tgt")
        col_top = lax.pmax(col_local, "src")
        row_total = lax.psum(jnp.sum(jnp.exp(scores - row_top[:, None]), axis=1), "tgt")
        col_total = lax.psum(jnp.sum(jnp.exp(scores - col_top[None, :]), axis=0), "src")
        row_weights = (jnp.exp(scores - row_top[:, None]) / row_total[:, None]).astype(jnp.bfloat16)
        col_weights = (jnp.exp(scores - col_top[None, :]) / col_total[None, :]).astype(jnp.bfloat16)
        source_sum, target_sum, target_full = translation_sums(
            row_weights, col_weights, source, target, share_target, src_index
        )
        covariance = jnp.dot(source_piece.T, source_sum, precision=highest)
        covariance = covariance + jnp.dot(target_sum.T, target_piece, precision=highest)
        covariance = lax.psum(covariance, ("src", "tgt"))
        current = polar_steps(covariance)
    source_share = source_sum.astype(jnp.bfloat16)
    target_soft = target_full.astype(jnp.bfloat16)
    return (source_share, target_soft, current)


def solution(mesh):
    in_specs = (P("src", None), P("tgt", None), P())
    out_specs = (P(("src", "tgt"), None), P("tgt", None), P())
    return jax.shard_map(body, mesh=mesh, in_specs=in_specs, out_specs=out_specs, check_vma=False)
```

profile of v0, /device:TPU:2, one launch (start us, length us, event | category | flops | bytes accessed | tf_op | source)
XLA Modules:
  0.0 1263.8 jit_solution(214851185553863919)
XLA Ops:
  9.3 7.3 multiply_reduce_fusion.2
  16.6 78.9 %pmax.29 = f32[2048]{0:T(1024)S(1)} all-reduce(f32[2048]{0:T(1024)S(1)} %get-tuple-element.9), channel_id=1, replica_groups=mesh['src'=32,'tgt'=8] {'src'}, use_global_device_ids=true, to_apply=%region_6.0 | all-reduce | flops 2048 | bytes 16384 | tf_op jit(solution)/shard_map/pmax | solution.py:71
  95.5 10.0 pmax.28
  105.6 5.2 fusion.1
  110.8 12.4 psum.56
  123.2 7.0 fusion.6
  130.3 70.6 %psum.57 = f32[2048]{0:T(1024)S(1)} all-reduce(f32[2048]{0:T(1024)S(1)} %get-tuple-element.7), channel_id=1, replica_groups=mesh['src'=32,'tgt'=8] {'src'}, use_global_device_ids=true, to_apply=%region_8.0 | all-reduce | flops 2048 | bytes 16384 | tf_op jit(solution)/shard_map/psum | solution.py:73
  201.0 7.6 fusion.4
  210.0 153.4 %all-reduce.5.cloned.1.call-done = f32[2048,300]{1,0:T(8,128)} async-done(((f32[2048,300]{1,0:T(8,128)}), f32[2048,300]{1,0:T(8,128)}) %all-reduce.5.cloned.1.call-update) | async-done | bytes 2457616 | tf_op jit(solution)/shard_map/psum | solution.py:27
  363.3 2.2 convolution_add_fusion.1
  365.8 248.9 %all-reduce.7.cloned.1.call-done = f32[300,300]{1,0:T(8,128)} async-done(((f32[300,300]{1,0:T(8,128)}), f32[300,300]{1,0:T(8,128)}) %all-reduce.7.cloned.1.call-update) | async-done | bytes 360016 | tf_op jit(solution)/shard_map/psum | solution.py:81
  614.7 1.7 multiply_reduce_fusion.5
  617.1 2.4 fusion.29
  619.5 2.2 fusion.25
  630.9 1.7 fusion.53
  638.2 5.3 multiply_reduce_fusion
  643.5 72.1 %pmax.31 = f32[2048]{0:T(1024)S(1)} all-reduce(f32[2048]{0:T(1024)S(1)} %get-tuple-element.5), channel_id=1, replica_groups=mesh['src'=32,'tgt'=8] {'src'}, use_global_device_ids=true, to_apply=%region_18.0 | all-reduce | flops 2048 | bytes 16384 | tf_op jit(solution)/shard_map/pmax | solution.py:71
  715.6 10.0 pmax.30
  725.6 5.2 fusion.3
  730.9 12.6 %psum.60 = f32[1024]{0:T(1024)S(1)} all-reduce(f32[1024]{0:T(1024)S(1)} %get-tuple-element.4), channel_id=1, replica_groups=mesh['src'=32,'tgt'=8] {'tgt'}, use_global_device_ids=true, to_apply=%region_15.0 | all-reduce | flops 1024 | bytes 8192 | tf_op jit(solution)/shard_map/psum | solution.py:72
  743.5 6.4 fusion.7
  750.0 70.8 %psum.61 = f32[2048]{0:T(1024)S(1)} all-reduce(f32[2048]{0:T(1024)S(1)} %get-tuple-element.3), channel_id=1, replica_groups=mesh['src'=32,'tgt'=8] {'src'}, use_global_device_ids=true, to_apply=%region_20.0 | all-reduce | flops 2048 | bytes 16384 | tf_op jit(solution)/shard_map/psum | solution.py:73
  820.8 6.8 fusion.5
  829.2 151.9 %all-reduce.9.cloned.1.call-done = f32[2048,300]{0,1:T(8,128)} async-done(((f32[2048,300]{0,1:T(8,128)}), f32[2048,300]{0,1:T(8,128)}) %all-reduce.9.cloned.1.call-update) | async-done | bytes 2457616 | tf_op jit(solution)/shard_map/psum | solution.py:27
  981.1 2.1 convolution_add_fusion
  983.2 1.6 convert_element_type.40
  984.8 2.9 convert_element_type.42
  987.7 244.7 %all-reduce.11.cloned.1.call-done = f32[300,300]{1,0:T(8,128)} async-done(((f32[300,300]{1,0:T(8,128)}), f32[300,300]{1,0:T(8,128)}) %all-reduce.11.cloned.1.call-update) | async-done | bytes 360016 | tf_op jit(solution)/shard_map/psum | solution.py:81
  1232.4 1.7 multiply_reduce_fusion.4
  1234.8 2.4 fusion.30
  1237.2 2.2 fusion.17
  1254.6 1.8 fusion.10
  (46 shorter events, 34.3 us)
Async XLA Ops:
  8.0 1.3 copy-start
  8.0 200.7 %reduce-scatter.3.cloned.1.call-start = ((), (), s32[]{:S(2)}) async-start(), calls=%async_computation.2 | async-start | bytes 1769472 | tf_op jit(solution)/shard_map/reduce_scatter | solution.py:21
  123.2 77.8 %copy-start.1 = (bf16[1024,300]{0,1:T(8,128)(2,1)S(1)}, bf16[1024,300]{0,1:T(8,128)(2,1)}, u32[]{:S(2)}) copy-start(bf16[1024,300]{0,1:T(8,128)(2,1)} %param.3) | copy-start | bytes 1843204
  130.3 233.1 %all-reduce.5.cloned.1.call-start = ((), (), s32[]{:S(2)}) async-start(), calls=%async_computation.3 | async-start | bytes 6291456 | tf_op jit(solution)/shard_map/psum | solution.py:27
  208.6 406.1 %all-reduce.7.cloned.1.call-start = ((), (), s32[]{:S(2)}) async-start(), calls=%async_computation.4 | async-start | bytes 933888 | tf_op jit(solution)/shard_map/psum | solution.py:81
  365.5 462.4 %reduce-scatter.5.cloned.1.call-start = ((), (), s32[]{:S(2)}) async-start(), calls=%async_computation.5 | async-start | bytes 1400832 | tf_op jit(solution)/shard_map/reduce_scatter | solution.py:21
  749.9 231.1 %all-reduce.9.cloned.1.call-start = ((), (), s32[]{:S(2)}) async-start(), calls=%async_computation.6 | async-start | bytes 4980736 | tf_op jit(solution)/shard_map/psum | solution.py:27
  827.7 404.7 %all-reduce.11.cloned.1.call-start = ((), (), s32[]{:S(2)}) async-start(), calls=%async_computation.7 | async-start | bytes 933888 | tf_op jit(solution)/shard_map/psum | solution.py:81
Sparse Core Ops, SparseCore 0:
  130.4 26.5 reduce-scatter.2
  365.6 248.9 all-reduce.6
  750.1 27.8 reduce-scatter.4
  983.3 249.0 all-reduce.10
Sparse Core Ops, SparseCore 1:
  208.7 154.6 all-reduce.4
  827.8 153.2 all-reduce.8
where the time goes:
time: 1270 us; the launch traced here: 1260 us
  waiting for transfers between devices  799 us (63%)
  blocking collectives  338 us (27%)
  matrix products  89.8 us (7%)
  other arithmetic  18.4 us (1%)
  between operations  17.2 us (1%)
    psum x2, waiting for transfers between devices, body(): covariance = lax.psum(covariance, ('src', 'tgt'))  494 us
    psum x2, waiting for transfers between devices, translation_sums(): lax.psum(lax.dot_general(col_weights, source, (((0,), (0,)), ((), ())), p...  305 us
    pmax x2, blocking collectives, body(): col_top = lax.pmax(col_local, 'src')  151 us
    psum x2, blocking collectives, body(): lax.psum(jnp.sum(jnp.exp(scores - col_top[None, :]), axis=0), 'src')  141 us
  transfers between devices with their start and end apart: 6, of which 4 were waited for; matrix products, arithmetic and copies ran while one was open for 2% of the time, Pallas kernels for 0%

commit v1 on v0

--- a/solution.py
+++ b/solution.py
@@ -78,7 +78,7 @@
         )
         covariance = jnp.dot(source_piece.T, source_sum, precision=highest)
         covariance = covariance + jnp.dot(target_sum.T, target_piece, precision=highest)
-        covariance = lax.psum(covariance, ("src", "tgt"))
+        covariance = lax.psum(lax.psum(covariance, "tgt"), "src")
         current = polar_steps(covariance)
     source_share = source_sum.astype(jnp.bfloat16)
     target_soft = target_full.astype(jnp.bfloat16)

time: 1270 us -> 1200 us (0.945)
  waiting for transfers between devices: 799 us -> 719 us
    psum x2 -> x4, waiting for transfers between devices: 494 us -> 413 us  [body(): covariance = lax.psum(lax.psum(covariance, 'tgt'), 'src')]
  transfers between devices with their start and end apart: 6 -> 8, of which waited for: 4 -> 6; matrix products, arithmetic and copies ran while one was open for 2% -> 2% of each run, Pallas kernels for 0% -> 0%
where the time goes in v1:
time: 1200 us
  waiting for transfers between devices  719 us (60%)
  blocking collectives  338 us (28%)
  matrix products  99.4 us (8%)
  other arithmetic  18.4 us (2%)
  between operations  17.7 us (1%)
    psum x4, waiting for transfers between devices, body(): covariance = lax.psum(lax.psum(covariance, 'tgt'), 'src')  413 us
    psum x2, waiting for transfers between devices, translation_sums(): lax.psum(lax.dot_general(col_weights, source, (((0,), (0,)), ((), ())), p...  306 us
    pmax x2, blocking collectives, body(): col_top = lax.pmax(col_local, 'src')  152 us
    psum x2, blocking collectives, body(): lax.psum(jnp.sum(jnp.exp(scores - col_top[None, :]), axis=0), 'src')  141 us
    dot_general x16, matrix products, polar_steps(): gram_matrix = jnp.dot(current.T, current, precision=highest)  32.4 us
    psum x2, blocking collectives, body(): lax.psum(jnp.sum(jnp.exp(scores - row_top[:, None]), axis=1), 'tgt')  24.8 us
  transfers between devices with their start and end apart: 8, of which 6 were waited for; matrix products, arithmetic and copies ran while one was open for 2% of the time, Pallas kernels for 0%

profile of v1, /device:TPU:2, one launch (start us, length us, event | category | flops | bytes accessed | tf_op | source)
XLA Modules:
  0.0 1195.1 jit_solution(2195208333994970090)
XLA Ops:
  9.3 7.3 multiply_reduce_fusion.2
  16.6 78.9 %pmax.29 = f32[2048]{0:T(1024)S(1)} all-reduce(f32[2048]{0:T(1024)S(1)} %get-tuple-element.9), channel_id=1, replica_groups=mesh['src'=32,'tgt'=8] {'src'}, use_global_device_ids=true, to_apply=%region_6.0 | all-reduce | flops 2048 | bytes 16384 | tf_op jit(solution)/shard_map/pmax | solution.py:71
  95.5 10.0 pmax.28
  105.6 5.2 fusion.1
  110.8 12.4 %psum.70 = f32[1024]{0:T(1024)S(1)} all-reduce(f32[1024]{0:T(1024)S(1)} %get-tuple-element.8), channel_id=1, replica_groups=mesh['src'=32,'tgt'=8] {'tgt'}, use_global_device_ids=true, to_apply=%region_3.0 | all-reduce | flops 1024 | bytes 8192 | tf_op jit(solution)/shard_map/psum | solution.py:72
  123.2 7.0 fusion.6
  130.3 70.6 %psum.71 = f32[2048]{0:T(1024)S(1)} all-reduce(f32[2048]{0:T(1024)S(1)} %get-tuple-element.7), channel_id=1, replica_groups=mesh['src'=32,'tgt'=8] {'src'}, use_global_device_ids=true, to_apply=%region_8.0 | all-reduce | flops 2048 | bytes 16384 | tf_op jit(solution)/shard_map/psum | solution.py:73
  201.0 7.6 fusion.4
  210.0 153.3 %all-reduce.7.cloned.1.call-done = f32[2048,300]{1,0:T(8,128)} async-done(((f32[2048,300]{1,0:T(8,128)}), f32[2048,300]{1,0:T(8,128)}) %all-reduce.7.cloned.1.call-update) | async-done | bytes 2457616 | tf_op jit(solution)/shard_map/psum | solution.py:27
  363.3 2.2 convolution_add_fusion.1
  365.5 60.0 %all-reduce.9.cloned.1.call-done = f32[300,300]{1,0:T(8,128)} async-done(((f32[300,300]{1,0:T(8,128)}), f32[300,300]{1,0:T(8,128)}) %all-reduce.9.cloned.1.call-update) | async-done | bytes 360016 | tf_op jit(solution)/shard_map/psum | solution.py:81
  425.8 148.8 %all-reduce.11.cloned.1.call-done = f32[300,300]{1,0:T(8,128)} async-done(((f32[300,300]{1,0:T(8,128)}), f32[300,300]{1,0:T(8,128)}) %all-reduce.11.cloned.1.call-update) | async-done | bytes 360016 | tf_op jit(solution)/shard_map/psum | solution.py:81
  574.6 1.7 multiply_reduce_fusion.5
  577.0 2.4 fusion.29
  579.4 2.2 fusion.25
  590.8 11.2 fusion.53
  607.7 5.3 multiply_reduce_fusion
  613.0 73.2 %pmax.31 = f32[2048]{0:T(1024)S(1)} all-reduce(f32[2048]{0:T(1024)S(1)} %get-tuple-element.5), channel_id=1, replica_groups=mesh['src'=32,'tgt'=8] {'src'}, use_global_device_ids=true, to_apply=%region_19.0 | all-reduce | flops 2048 | bytes 16384 | tf_op jit(solution)/shard_map/pmax | solution.py:71
  686.3 10.0 pmax.30
  696.3 5.2 fusion.3
  701.5 12.4 %psum.75 = f32[1024]{0:T(1024)S(1)} all-reduce(f32[1024]{0:T(1024)S(1)} %get-tuple-element.4), channel_id=1, replica_groups=mesh['src'=32,'tgt'=8] {'tgt'}, use_global_device_ids=true, to_apply=%region_16.0 | all-reduce | flops 1024 | bytes 8192 | tf_op jit(solution)/shard_map/psum | solution.py:72
  714.0 6.4 fusion.7
  720.5 70.6 %psum.76 = f32[2048]{0:T(1024)S(1)} all-reduce(f32[2048]{0:T(1024)S(1)} %get-tuple-element.3), channel_id=1, replica_groups=mesh['src'=32,'tgt'=8] {'src'}, use_global_device_ids=true, to_apply=%region_21.0 | all-reduce | flops 2048 | bytes 16384 | tf_op jit(solution)/shard_map/psum | solution.py:73
  791.1 6.8 fusion.5
  799.3 152.6 %all-reduce.13.cloned.1.call-done = f32[2048,300]{0,1:T(8,128)} async-done(((f32[2048,300]{0,1:T(8,128)}), f32[2048,300]{0,1:T(8,128)}) %all-reduce.13.cloned.1.call-update) | async-done | bytes 2457616 | tf_op jit(solution)/shard_map/psum | solution.py:27
  951.9 2.1 convolution_add_fusion
  954.3 59.9 %all-reduce.15.cloned.1.call-done = f32[300,300]{1,0:T(8,128)} async-done(((f32[300,300]{1,0:T(8,128)}), f32[300,300]{1,0:T(8,128)}) %all-reduce.15.cloned.1.call-update) | async-done | bytes 360016 | tf_op jit(solution)/shard_map/psum | solution.py:81
  1015.7 2.9 convert_element_type.42
  1018.6 144.6 %all-reduce.17.cloned.1.call-done = f32[300,300]{1,0:T(8,128)} async-done(((f32[300,300]{1,0:T(8,128)}), f32[300,300]{1,0:T(8,128)}) %all-reduce.17.cloned.1.call-update) | async-done | bytes 360016 | tf_op jit(solution)/shard_map/psum | solution.py:81
  1165.6 2.4 fusion.30
  1168.0 2.2 fusion.17
  1185.5 1.8 fusion.10
  (52 shorter events, 37.9 us)
Async XLA Ops:
  8.0 1.3 copy-start
  8.0 200.7 %reduce-scatter.3.cloned.1.call-start = ((), (), s32[]{:S(2)}) async-start(), calls=%async_computation.2 | async-start | bytes 1769472 | tf_op jit(solution)/shard_map/reduce_scatter | solution.py:21
  123.2 77.8 %copy-start.1 = (bf16[1024,300]{0,1:T(8,128)(2,1)S(1)}, bf16[1024,300]{0,1:T(8,128)(2,1)}, u32[]{:S(2)}) copy-start(bf16[1024,300]{0,1:T(8,128)(2,1)} %param.3) | copy-start | bytes 1843204
  130.3 233.0 %all-reduce.7.cloned.1.call-start = ((), (), s32[]{:S(2)}) async-start(), calls=%async_computation.3 | async-start | bytes 6291456 | tf_op jit(solution)/shard_map/psum | solution.py:27
  208.6 216.9 %all-reduce.9.cloned.1.call-start = ((), (), s32[]{:S(2)}) async-start(), calls=%async_computation.4 | async-start | bytes 933888 | tf_op jit(solution)/shard_map/psum | solution.py:81
  365.5 209.1 %all-reduce.11.cloned.1.call-start = ((), (), s32[]{:S(2)}) async-start(), calls=%async_computation.5 | async-start | bytes 933888 | tf_op jit(solution)/shard_map/psum | solution.py:81
  425.5 372.5 %reduce-scatter.5.cloned.1.call-start = ((), (), s32[]{:S(2)}) async-start(), calls=%async_computation.6 | async-start | bytes 1400832 | tf_op jit(solution)/shard_map/reduce_scatter | solution.py:21
  720.4 231.5 %all-reduce.13.cloned.1.call-start = ((), (), s32[]{:S(2)}) async-start(), calls=%async_computation.7 | async-start | bytes 4980736 | tf_op jit(solution)/shard_map/psum | solution.py:27
  798.0 216.2 %all-reduce.15.cloned.1.call-start = ((), (), s32[]{:S(2)}) async-start(), calls=%async_computation.8 | async-start | bytes 933888 | tf_op jit(solution)/shard_map/psum | solution.py:81
  954.0 209.2 %all-reduce.17.cloned.1.call-start = ((), (), s32[]{:S(2)}) async-start(), calls=%async_computation.9 | async-start | bytes 933888 | tf_op jit(solution)/shard_map/psum | solution.py:81
Sparse Core Ops, SparseCore 0:
  130.4 26.5 reduce-scatter.2
  365.6 59.8 all-reduce.8
  720.5 28.2 reduce-scatter.4
  954.1 59.9 all-reduce.14
Sparse Core Ops, SparseCore 1:
  208.7 154.5 all-reduce.6
  425.6 148.9 all-reduce.10
  798.1 153.8 all-reduce.12
  1014.2 148.9 all-reduce.16
